TPU v7x, 512 devices: a whole 4x4x16 slice. The times are simulated.
512 devices in a mesh: grp: 64 (over z, y), seq: 8 (over x, core).
Axes of the slice: x: 4, y: 4, z: 16, core: 2. Of those that a mesh axis runs over, the one named last changes fastest.
Arguments:
- tokens: bfloat16 [64, 1024, 2048], P('grp', 'seq'), may hold values from -6 to 6
- seg_ids: int32 [64, 1024], P('grp'), may hold values from 0 to 3, never falling along the last dimension, each value on 1 to 512 neighbouring positions
- deal: int32 [64, 1024], P('grp'), may hold values from 0 to 1023, each once within a row
- page_table: int32 [64, 128], P('grp'), may hold values from 0 to 127, each once within a row
- in_gain: float32 [2048], replicated, may hold values from 0.1 to 1.9
- w_query: bfloat16 [2048, 2048], P('grp', 'seq'), may hold values from -0.125 to 0.125
- key_projection_weight: bfloat16 [2048, 512], P('grp'), may hold values from -0.125 to 0.125
- value_projection_weight: bfloat16 [2048, 512], P('grp'), may hold values from -0.125 to 0.125
- q_gain: float32 [256], replicated, may hold values from 1.25 to 3.75
- key_norm_gain: float32 [256], replicated, may hold values from 0.1 to 1.9
- w_out: bfloat16 [2048, 2048], P('seq', 'grp'), may hold values from -0.125 to 0.125
- post_gain: float32 [2048], replicated, may hold values from 0.1 to 1.9
- final_gain: float32 [2048], replicated, may hold values from 0.1 to 1.9
- embed: bfloat16 [262144, 2048], P(('grp', 'seq')), may hold values from -0.375 to 0.375
Outputs:
- hidden_out: bfloat16 [64, 1024, 2048], P('grp', 'seq')
- kv_cache: bfloat16 [64, 128, 8, 1024], P('grp', 'seq')
- last_norm: float32 [256], replicated
- max_logit: float32 [256], replicated
Inputs may be any that keep to these rules, and one draw needn't show every extreme that they name: `seg_ids`: along each pack the prompt numbers never fall; every one of the 4 prompts occurs, none has more than 512 positions, and one has exactly that many. Each row of deal holds every packed position once. Each row of page_table holds every page of the pack once.
All inputs are finite; a program needn't handle non-finite values.
Results may differ from a plain program's by a relative error of at most 0.015.
The roundings to bfloat16 on the way count: a program that leaves them out, or rounds other values in their place, can miss the bound.
Values may be sent and summed in bfloat16 or wider, within the bound.
A program may use at most 64 MiB of HBM per device.

v0:
```python
import jax
import jax.numpy as jnp
from jax import lax
from jax.sharding import PartitionSpec as P

QUERY_HEADS = 8
KEY_HEADS = 2
PAGE_SLOTS = 8
SEGS = 4
eps = 1e-06
rope_base = 1000000.0
cap_value = 30.0


def rows_scaled(value_rows, scales):
    mean_square = jnp.mean(value_rows * value_rows, axis=-1, keepdims=True)
    return value_rows * lax.rsqrt(mean_square + eps) * scales


def rotate(value_rows, offsets):
    half_width = value_rows.shape[-1] // 2
    frequency = rope_base ** (
        -2.0 * jnp.arange(half_width, dtype=jnp.float32) / value_rows.shape[-1]
    )
    angles = offsets.astype(jnp.float32)[:, None] * frequency[None, :]
    cosine = jnp.cos(angles)[:, None, :]
    sine_table = jnp.sin(angles)[:, None, :]
    lower_half = value_rows[..., :half_width]
    upper_half = value_rows[..., half_width:]
    return jnp.concatenate(
        [
            lower_half * cosine - upper_half * sine_table,
            upper_half * cosine + lower_half * sine_table,
        ],
        axis=-1,
    )


def layout(segment, dealing):
    row_seg = jnp.take(segment, dealing)
    before = jnp.sum((segment[None, :] < row_seg[:, None]).astype(jnp.int32), axis=1)
    return (row_seg, dealing - before)


def attend(query, key_selected, value_selected, row_seg, dealing):
    scores = jnp.einsum("qhd,khd->hqk", query, key_selected, preferred_element_type=jnp.float32)
    allowed = (row_seg[:, None] == row_seg[None, :]) & (dealing[None, :] <= dealing[:, None])
    masked = jnp.where(allowed[None], scores, -1e30)
    row_peak = jnp.max(masked, axis=-1, keepdims=True)
    raw_weights = jnp.where(allowed[None], jnp.exp(masked - row_peak), 0.0)
    row_total = jnp.sum(raw_weights, axis=-1, keepdims=True)
    weights = (raw_weights / row_total).astype(jnp.bfloat16)
    attended = jnp.einsum(
        "hqk,khd->qhd", weights, value_selected, preferred_element_type=jnp.float32
    )
    return attended.astype(jnp.bfloat16).reshape(query.shape[0], -1)


def shards(
    tokens,
    seg_ids,
    deal,
    page_table,
    in_gain,
    w_query,
    key_projection_weight,
    value_projection_weight,
    q_gain,
    key_norm_gain,
    w_out,
    post_gain,
    final_gain,
    embed,
):
    own_tokens = tokens[0]
    rows_dev = own_tokens.shape[0]
    segment = seg_ids[0]
    dealing = deal[0]
    width_of_head = q_gain.shape[0]
    heads_local = w_query.shape[1] // width_of_head
    sequence_index = lax.axis_index("seq")
    own_start = sequence_index * rows_dev
    row_seg, offsets = layout(segment, dealing)
    normed_own = rows_scaled(own_tokens.astype(jnp.float32), in_gain).astype(jnp.bfloat16)
    normed_all = lax.all_gather(normed_own, "seq", axis=0, tiled=True)
    rows_of_pack = normed_all.shape[0]
    key_value_offsets = lax.dynamic_slice_in_dim(offsets, own_start, rows_dev, 0)
    query_full, key_full, value_full, out_full = (
        lax.all_gather(w_query, "grp", axis=0, tiled=True),
        lax.all_gather(key_projection_weight, "grp", axis=0, tiled=True),
        lax.all_gather(value_projection_weight, "grp", axis=0, tiled=True),
        lax.all_gather(w_out, "grp", axis=1, tiled=True),
    )
    query_raw = jnp.dot(normed_all, query_full, preferred_element_type=jnp.float32)
    key_unnormed = jnp.dot(normed_own, key_full, preferred_element_type=jnp.float32)
    value_unnormed = jnp.dot(normed_own, value_full, preferred_element_type=jnp.float32)
    query = rotate(
        rows_scaled(query_raw.reshape(rows_of_pack, heads_local, width_of_head), q_gain), offsets
    ).astype(jnp.bfloat16)
    rows_of_source = normed_own.shape[0]
    key_local_part = rotate(
        rows_scaled(key_unnormed.reshape(rows_of_source, KEY_HEADS, width_of_head), key_norm_gain),
        key_value_offsets,
    ).astype(jnp.bfloat16)
    value_local_part = rows_scaled(
        value_unnormed.reshape(rows_of_source, KEY_HEADS, width_of_head), 1.0
    ).astype(jnp.bfloat16)
    key_local_part = key_local_part.reshape(rows_of_source, KEY_HEADS * width_of_head)
    value_local_part = value_local_part.reshape(rows_of_source, KEY_HEADS * width_of_head)
    key_gathered, value_gathered = (
        lax.all_gather(key_local_part, "seq", axis=0, tiled=True),
        lax.all_gather(value_local_part, "seq", axis=0, tiled=True),
    )
    index_of_head = (sequence_index * heads_local + jnp.arange(heads_local, dtype=jnp.int32)) // (
        QUERY_HEADS // KEY_HEADS
    )
    key_selected = jnp.take(
        key_gathered.reshape(rows_of_pack, KEY_HEADS, width_of_head), index_of_head, axis=1
    )
    value_selected = jnp.take(
        value_gathered.reshape(rows_of_pack, KEY_HEADS, width_of_head), index_of_head, axis=1
    )
    attended = attend(query, key_selected, value_selected, row_seg, dealing)
    partial_out = jnp.dot(attended, out_full, preferred_element_type=jnp.float32)
    summed = lax.psum_scatter(
        partial_out.astype(jnp.bfloat16), "seq", scatter_dimension=0, tiled=True
    ).astype(jnp.float32)
    hidden = (own_tokens.astype(jnp.float32) + rows_scaled(summed, post_gain)).astype(jnp.bfloat16)
    inverse_assignment = jnp.argsort(dealing)
    inverse_page = jnp.argsort(page_table[0])
    own_pages = rows_dev // PAGE_SLOTS
    physical = sequence_index * own_pages + jnp.arange(own_pages, dtype=jnp.int32)
    logical_index = jnp.take(inverse_page, physical)
    packed = logical_index[:, None] * PAGE_SLOTS + jnp.arange(PAGE_SLOTS, dtype=jnp.int32)[None, :]
    source_index = jnp.take(inverse_assignment, packed.reshape(-1))
    stacked_rows = jnp.concatenate([key_gathered, value_gathered], axis=1)
    cache_pages = jnp.take(stacked_rows, source_index, axis=0).reshape(
        own_pages, PAGE_SLOTS, stacked_rows.shape[1]
    )
    last_pos = (
        jnp.sum(
            (segment[None, :] <= jnp.arange(SEGS, dtype=jnp.int32)[:, None]).astype(jnp.int32),
            axis=1,
        )
        - 1
    )
    local_row = jnp.take(inverse_assignment, last_pos) - own_start
    selector = (local_row[:, None] == jnp.arange(rows_dev, dtype=jnp.int32)[None, :]).astype(
        jnp.bfloat16
    )
    group_states = jnp.dot(selector, hidden, preferred_element_type=jnp.float32)
    pack_states = lax.psum(group_states.astype(jnp.bfloat16), "seq")
    states = lax.all_gather(pack_states, "grp", axis=0, tiled=True).astype(jnp.float32)
    last_norm = jnp.sqrt(jnp.mean(states * states, axis=-1))
    final = rows_scaled(states, final_gain).astype(jnp.bfloat16)
    logits = lax.dot_general(
        final, embed, (((1,), (1,)), ((), ())), preferred_element_type=jnp.float32
    )
    shard_max = jnp.max(cap_value * jnp.tanh(logits / cap_value), axis=1)
    max_logit = lax.pmax(shard_max, ("grp", "seq"))
    return (hidden[None], cache_pages[None], last_norm, max_logit)


def solution(mesh):
    return jax.shard_map(
        shards,
        mesh=mesh,
        in_specs=(
            P("grp", "seq", None),
            P("grp", None),
            P("grp", None),
            P("grp", None),
            P(),
            P("grp", "seq"),
            P("grp", None),
            P("grp", None),
            P(),
            P(),
            P("seq", "grp"),
            P(),
            P(),
            P(("grp", "seq"), None),
        ),
        out_specs=(P("grp", "seq", None), P("grp", "seq", None, None), P(), P()),
        check_vma=False,
    )
```

profile of v0, /device:TPU:1, one launch (start us, length us, event | category | flops | bytes accessed | tf_op | source)
XLA Modules:
  0.0 1011.3 jit_solution(3232940448721086610)
XLA Ops:
  7.3 0.7 all-gather.18.cloned.1.call-update
  8.0 0.7 all-gather.10.cloned.1.call-update
  8.7 0.7 compare_select_fusion.1
  9.5 5.7 gather_fusion
  16.3 132.1 %all-gather.18.cloned.1.call-done = bf16[2048,512]{1,0:T(8,128)(2,1)} async-done(((bf16[32,512]{1,0:T(8,128)(2,1)}), bf16[2048,512]{1,0:T(8,128)(2,1)}) %all-gather.18.cloned.1.call-update) | async-done | bytes 2097168 | tf_op jit(solution)/shard_map/all_gather | solution.py:90
  148.5 3.9 copy.40
  152.4 2.5 multiply_reduce_fusion.2
  155.2 0.8 copy.42
  156.1 132.3 %all-gather.10.cloned.1.call-done = bf16[2048,512]{1,0:T(8,128)(2,1)} async-done(((bf16[32,512]{1,0:T(8,128)(2,1)}), bf16[2048,512]{1,0:T(8,128)(2,1)}) %all-gather.10.cloned.1.call-update) | async-done | bytes 2097168 | tf_op jit(solution)/shard_map/all_gather | solution.py:91
  288.4 4.0 copy.36
  292.4 2.5 multiply_reduce_fusion.3
  295.1 0.8 copy.38
  296.6 1.0 fusion.15
  297.6 0.7 all-gather.22.cloned.1.call-update
  298.6 29.0 %all-gather.20.cloned.1.call-done = bf16[1024,512]{1,0:T(8,128)(2,1)} async-done(((bf16[128,512]{1,0:T(8,128)(2,1)}), bf16[1024,512]{1,0:T(8,128)(2,1)}) %all-gather.20.cloned.1.call-update) | async-done | bytes 1048592 | tf_op jit(solution)/shard_map/all_gather | solution.py:111
  327.6 2.2 reshape.529
  329.8 3.3 constant_dynamic-slice_fusion
  333.1 27.5 %all-gather.12.cloned.1.call-done = bf16[1024,512]{1,0:T(8,128)(2,1)} async-done(((bf16[128,512]{1,0:T(8,128)(2,1)}), bf16[1024,512]{1,0:T(8,128)(2,1)}) %all-gather.12.cloned.1.call-update) | async-done | bytes 1048592 | tf_op jit(solution)/shard_map/all_gather | solution.py:112
  360.6 2.2 reshape.527
  362.8 3.3 constant_dynamic-slice_fusion.1
  366.1 126.2 %all-gather.16.cloned.1.call-done = bf16[2048,256]{1,0:T(8,128)(2,1)} async-done(((bf16[32,256]{1,0:T(8,128)(2,1)}), bf16[2048,256]{1,0:T(8,128)(2,1)}) %all-gather.16.cloned.1.call-update) | async-done | bytes 1048592 | tf_op jit(solution)/shard_map/all_gather | solution.py:89
  492.3 48.3 %all-gather.14.cloned.1.call-done = bf16[1024,2048]{1,0:T(8,128)(2,1)} async-done(((bf16[128,2048]{1,0:T(8,128)(2,1)}), bf16[1024,2048]{1,0:T(8,128)(2,1)}) %all-gather.14.cloned.1.call-update) | async-done | bytes 4194320 | tf_op jit(solution)/shard_map/all_gather | solution.py:85
  540.6 3.9 multiply_reduce_fusion.1
  544.7 2.3 fusion.46
  547.0 1.0 fusion.1
  548.0 2.0 copy-done.3
  550.0 1.5 fusion.64
  551.5 121.2 %all-gather.22.cloned.1.call-done = bf16[256,2048]{0,1:T(8,128)(2,1)} async-done(((bf16[256,32]{0,1:T(8,128)(2,1)}), bf16[256,2048]{0,1:T(8,128)(2,1)}) %all-gather.22.cloned.1.call-update) | async-done | bytes 1048592 | tf_op jit(solution)/shard_map/all_gather | solution.py:92
  672.7 7.6 convolution_convert_fusion
  680.4 4.4 sort.35
  684.8 2.5 sort.34
  687.3 0.7 gather_fusion.1
  688.1 0.6 gather_fusion.4
  688.8 40.6 %reduce-scatter.2.cloned.1.call-done = bf16[128,2048]{1,0:T(8,128)(2,1)} async-done(((bf16[1024,2048]{1,0:T(8,128)(2,1)}), bf16[128,2048]{1,0:T(8,128)(2,1)}) %reduce-scatter.2.cloned.1.call-update) | async-done | bytes 524304 | tf_op jit(solution)/shard_map/reduce_scatter | solution.py:125
  729.4 1.2 fusion.11
  730.6 1.5 convolution_convert_fusion.1
  732.1 24.1 %psum.7 = bf16[4,2048]{1,0:T(4,128)(2,1)} all-reduce(bf16[4,2048]{1,0:T(4,128)(2,1)S(1)} %convolution_convert_fusion.1), channel_id=1, replica_groups=mesh['grp'=64,'seq'=8] {'seq'}, use_global_device_ids=true, to_apply=%region_12.14 | all-reduce | flops 8192 | bytes 32768 | tf_op jit(solution)/shard_map/psum | solution.py:152
  756.4 1.0 gather_fusion.2
  757.6 3.2 pad_maximum_fusion
  760.8 2.9 gather_fusion.3
  763.7 0.8 bitcast_select_fusion
  764.5 1.1 fusion.63
  765.5 121.9 %all-gather.24.cloned.1.call-done = bf16[64,4,2048]{2,1,0:T(4,128)(2,1)} async-done(((bf16[1,4,2048]{2,1,0:T(4,128)(2,1)}), bf16[64,4,2048]{2,1,0:T(4,128)(2,1)}) %all-gather.24.cloned.1.call-update) | async-done | bytes 1048592 | tf_op jit(solution)/shard_map/all_gather | solution.py:153
  887.5 2.5 reshape.630
  890.0 1.8 multiply_reduce_fusion
  891.8 0.6 add_rsqrt_fusion.1
  892.3 2.4 fusion.10
  894.8 110.0 %pmax.7 = f32[256]{0:T(256)} all-reduce(f32[256]{0:T(256)S(1)} %fusion.10), channel_id=1, replica_groups=mesh['grp'=64,'seq'=8] {'grp','seq'}, use_global_device_ids=true, to_apply=%region_15.17 | all-reduce | flops 256 | bytes 2048 | tf_op jit(solution)/shard_map/pmax | solution.py:160
  (78 shorter events, 3.6 us)
Async XLA Ops:
  7.2 885.2 %copy-start = (bf16[512,2048]{1,0:T(8,128)(2,1)S(1)}, bf16[512,2048]{1,0:T(8,128)(2,1)}, u32[]{:S(2)}) copy-start(bf16[512,2048]{1,0:T(8,128)(2,1)} %param.29) | copy-start | bytes 6291460
  7.2 8.0 copy-start.6
  7.2 8.1 copy-start.1
  7.2 8.6 copy-start.2
  7.2 141.2 %all-gather.18.cloned.1.call-start = ((), (), s32[]{:S(2)}) async-start(), calls=%async_computation.5 | async-start | bytes 2129920 | tf_op jit(solution)/shard_map/all_gather | solution.py:90
  7.9 280.5 %all-gather.10.cloned.1.call-start = ((), (), s32[]{:S(2)}) async-start(), calls=%async_computation.1 | async-start | bytes 2129920 | tf_op jit(solution)/shard_map/all_gather | solution.py:91
  8.7 318.9 %all-gather.20.cloned.1.call-start = ((), (), s32[]{:S(2)}) async-start(), calls=%async_computation.6 | async-start | bytes 1179648 | tf_op jit(solution)/shard_map/all_gather | solution.py:111
  9.4 143.0 %copy-start.7 = (f32[2048]{0:T(1024)S(1)}, f32[2048]{0:T(1024)}, u32[]{:S(2)}) copy-start(f32[2048]{0:T(1024)} %param.20) | copy-start | bytes 24580
  15.2 139.7 %copy-start.9 = (f32[256]{0:T(256)S(1)}, f32[256]{0:T(256)}, u32[]{:S(2)}) copy-start(f32[256]{0:T(256)} %param.25) | copy-start | bytes 3076
  156.0 204.6 %all-gather.12.cloned.1.call-start = ((), (), s32[]{:S(2)}) async-start(), calls=%async_computation.2 | async-start | bytes 1179648 | tf_op jit(solution)/shard_map/all_gather | solution.py:112
  295.9 196.3 %all-gather.16.cloned.1.call-start = ((), (), s32[]{:S(2)}) async-start(), calls=%async_computation.4 | async-start | bytes 1064960 | tf_op jit(solution)/shard_map/all_gather | solution.py:89
  296.5 244.1 %all-gather.14.cloned.1.call-start = ((), (), s32[]{:S(2)}) async-start(), calls=%async_computation.3 | async-start | bytes 4718592 | tf_op jit(solution)/shard_map/all_gather | solution.py:85
  297.6 375.1 %all-gather.22.cloned.1.call-start = ((), (), s32[]{:S(2)}) async-start(), calls=%async_computation.7 | async-start | bytes 1064960 | tf_op jit(solution)/shard_map/all_gather | solution.py:92
  298.3 431.1 %reduce-scatter.2.cloned.1.call-start = ((), (), s32[]{:S(2)}) async-start(), calls=%async_computation.8 | async-start | bytes 4718592 | tf_op jit(solution)/shard_map/reduce_scatter | solution.py:125
  366.1 178.5 %copy-start.10 = (f32[256]{0:T(256)S(1)}, f32[256]{0:T(256)}, u32[]{:S(2)}) copy-start(f32[256]{0:T(256)} %param.24) | copy-start | bytes 3076
  540.6 6.4 copy-start.5
  548.0 2.0 copy-start.3
  680.3 4.5 copy-start.12
  680.3 50.3 %copy-start.8 = (f32[2048]{0:T(1024)S(1)}, f32[2048]{0:T(1024)}, u32[]{:S(2)}) copy-start(f32[2048]{0:T(1024)} %param.27) | copy-start | bytes 24580
  680.3 207.2 %all-gather.24.cloned.1.call-start = ((), (), s32[]{:S(2)}) async-start(), calls=%async_computation.9 | async-start | bytes 1064960 | tf_op jit(solution)/shard_map/all_gather | solution.py:153
  730.6 33.9 %copy-start.4 = (bf16[128,2048]{1,0:T(8,128)(2,1)S(1)}, bf16[128,2048]{1,0:T(8,128)(2,1)}, u32[]{:S(2)}) copy-start(bf16[128,2048]{1,0:T(8,128)(2,1)} %reduce-scatter.2.cloned.1.call-done) | copy-start | bytes 1572868
  763.7 128.7 %copy-start.11 = (f32[2048]{0:T(1024)S(1)}, f32[2048]{0:T(1024)}, u32[]{:S(2)}) copy-start(f32[2048]{0:T(1024)} %param.28) | copy-start | bytes 24580
Sparse Core Ops, SparseCore 0:
  11.0 137.4 all-gather.17
  151.4 136.9 all-gather.9
  291.1 36.4 all-gather.19
  329.6 30.9 all-gather.11
  363.4 128.8 all-gather.15
  494.8 45.7 all-gather.13
  543.6 129.0 all-gather.21
  680.5 48.8 reduce-scatter.1
  756.3 131.0 all-gather.23
where the time goes:
time: 1010 us
  waiting for transfers between devices  782 us (77%)
  blocking collectives  134 us (13%)
  local copies, waits for them, and re-layouts  36.2 us (4%)
  other arithmetic  22.9 us (2%)
  matrix products  21.4 us (2%)
  between operations  14.2 us (1%)
    all_gather x1, waiting for transfers between devices, shards(): lax.all_gather(value_projection_weight, 'grp', axis=0, tiled=True)  132 us
    all_gather x1, waiting for transfers between devices, shards(): lax.all_gather(key_projection_weight, 'grp', axis=0, tiled=True)  132 us
    all_gather x1, waiting for transfers between devices, shards(): lax.all_gather(w_query, 'grp', axis=0, tiled=True)  126 us
    all_gather x1, waiting for transfers between devices, shards(): lax.all_gather(pack_states, 'grp', axis=0, tiled=True).astype(jnp.float32)  122 us
    all_gather x1, waiting for transfers between devices, shards(): lax.all_gather(w_out, 'grp', axis=1, tiled=True)  121 us
    pmax x1, blocking collectives, shards(): max_logit = lax.pmax(shard_max, ('grp', 'seq'))  110 us
    all_gather x1, waiting for transfers between devices, shards(): normed_all = lax.all_gather(normed_own, 'seq', axis=0, tiled=True)  48.3 us
    reduce_scatter x1, waiting for transfers between devices, shards(): lax.psum_scatter(partial_out.astype(jnp.bfloat16), 'seq', scatter_dimensi...  40.6 us
  transfers between devices with their start and end apart: 9, of which 9 were waited for; matrix products, arithmetic and copies ran while one was open for 6% of the time, Pallas kernels for 0%

commit v1 on v0

--- a/solution.py
+++ b/solution.py
@@ -10,6 +10,28 @@
 eps = 1e-06
 rope_base = 1000000.0
 cap_value = 30.0
+
+
+def laid_out(blocks, dim):
+    blocks = jnp.moveaxis(blocks, 0, dim)
+    shape = blocks.shape
+    return blocks.reshape(*shape[:dim], shape[dim] * shape[dim + 1], *shape[dim + 2 :])
+
+
+def collect(shard, axis, dim):
+    size = lax.axis_size(axis)
+    pairs = [(i, (i + 1) % size) for i in range(size)]
+    back = [(b, a) for a, b in pairs]
+    lower, upper = ([], [])
+    for step in range(size - 1):
+        if step % 2 == 0:
+            lower.append(lax.ppermute(lower[-1] if lower else shard, axis, pairs))
+        else:
+            upper.append(lax.ppermute(upper[-1] if upper else shard, axis, back))
+    blocks = jnp.stack([*lower[::-1], shard, *upper])
+    shift = lax.axis_index(axis) - len(lower)
+    blocks = blocks[(jnp.arange(size) - shift) % size]
+    return laid_out(blocks, dim)
 
 
 def rows_scaled(value_rows, scales):
@@ -82,7 +104,7 @@
     own_start = sequence_index * rows_dev
     row_seg, offsets = layout(segment, dealing)
     normed_own = rows_scaled(own_tokens.astype(jnp.float32), in_gain).astype(jnp.bfloat16)
-    normed_all = lax.all_gather(normed_own, "seq", axis=0, tiled=True)
+    normed_all = collect(normed_own, "seq", 0)
     rows_of_pack = normed_all.shape[0]
     key_value_offsets = lax.dynamic_slice_in_dim(offsets, own_start, rows_dev, 0)
     query_full, key_full, value_full, out_full = (

time: 1010 us -> 970 us (0.960)
  waiting for transfers between devices: 782 us -> 701 us
  starting transfers between devices: 0.54 us -> 22.6 us
  local copies, waits for them, and re-layouts: 36.2 us -> 52.1 us
    all_gather x1, waiting for transfers between devices: 126 us -> 68.6 us  [shards(): lax.all_gather(w_query, 'grp', axis=0, tiled=True)]
    all_gather x1 -> x0, waiting for transfers between devices: 48.3 us -> none  [shards(): normed_all = lax.all_gather(normed_own, 'seq', axis=0, tiled=True)]
    ppermute x0 -> x7, starting transfers between devices: none -> 22.1 us  [the longest x4 18.2 us: collect(): lower.append(lax.ppermute(lower[-1] if lower else shard, axis, pairs))]
    ppermute x0 -> x7, waiting for transfers between devices: none -> 20.6 us  [the longest x4 20.4 us: collect(): lower.append(lax.ppermute(lower[-1] if lower else shard, axis, pairs))]
    unnamed x26 -> x32, local copies, waits for them, and re-layouts: 2.02 us -> 13.1 us
  transfers between devices with their start and end apart: 9 -> 15, of which waited for: 9 -> 13; matrix products, arithmetic and copies ran while one was open for 6% -> 8% of each run, Pallas kernels for 0% -> 0%
where the time goes in v1:
time: 970 us; the launch traced here: 969 us
  waiting for transfers between devices  701 us (72%)
  blocking collectives  134 us (14%)
  local copies, waits for them, and re-layouts  52.1 us (5%)
  other arithmetic  23.8 us (2%)
  starting transfers between devices  22.6 us (2%)
  matrix products  21.3 us (2%)
  between operations  14.6 us (2%)
    all_gather x1, waiting for transfers between devices, shards(): lax.all_gather(value_projection_weight, 'grp', axis=0, tiled=True)  132 us
    all_gather x1, waiting for transfers between devices, shards(): lax.all_gather(key_projection_weight, 'grp', axis=0, tiled=True)  131 us
    all_gather x1, waiting for transfers between devices, shards(): lax.all_gather(pack_states, 'grp', axis=0, tiled=True).astype(jnp.float32)  122 us
    all_gather x1, waiting for transfers between devices, shards(): lax.all_gather(w_out, 'grp', axis=1, tiled=True)  119 us
    pmax x1, blocking collectives, shards(): max_logit = lax.pmax(shard_max, ('grp', 'seq'))  110 us
    all_gather x1, waiting for transfers between devices, shards(): lax.all_gather(w_query, 'grp', axis=0, tiled=True)  68.6 us
    reduce_scatter x1, waiting for transfers between devices, shards(): lax.psum_scatter(partial_out.astype(jnp.bfloat16), 'seq', scatter_dimensi...  40.8 us
    all_gather x1, waiting for transfers between devices, shards(): lax.all_gather(key_local_part, 'seq', axis=0, tiled=True)  33.4 us
  transfers between devices with their start and end apart: 15, of which 13 were waited for; matrix products, arithmetic and copies ran while one was open for 8% of the time, Pallas kernels for 0%

profile of v1, /device:TPU:1, one launch (start us, length us, event | category | flops | bytes accessed | tf_op | source)
XLA Modules:
  0.0 969.2 jit_solution(7155582218756838344)
XLA Ops:
  11.0 5.7 gather_fusion
  17.9 130.6 %all-gather.15.cloned.1.call-done = bf16[2048,512]{1,0:T(8,128)(2,1)} async-done(((bf16[32,512]{1,0:T(8,128)(2,1)}), bf16[2048,512]{1,0:T(8,128)(2,1)}) %all-gather.15.cloned.1.call-update) | async-done | bytes 2097168 | tf_op jit(solution)/shard_map/all_gather | solution.py:112
  148.5 3.9 copy.40
  152.4 2.5 multiply_reduce_fusion.2
  156.1 132.3 %all-gather.9.cloned.1.call-done = bf16[2048,512]{1,0:T(8,128)(2,1)} async-done(((bf16[32,512]{1,0:T(8,128)(2,1)}), bf16[2048,512]{1,0:T(8,128)(2,1)}) %all-gather.9.cloned.1.call-update) | async-done | bytes 2097168 | tf_op jit(solution)/shard_map/all_gather | solution.py:113
  288.4 4.0 copy.36
  292.4 2.5 multiply_reduce_fusion.3
  296.2 10.6 %collective-permute-start = (bf16[128,2048]{1,0:T(8,128)(2,1)S(1)}, bf16[128,2048]{1,0:T(8,128)(2,1)S(1)}, u32[]{:S(2)}, u32[]{:S(2)}) collective-permute-start(bf16[128,2048]{1,0:T(8,128)(2,1)S(1)} %fusion.15), channel_id=1, source_target_pairs={{0,1},{1,2},{2,3},{3,4},{4,5},{5,6},{6,7},{7,0},{8,9},{9,10},{10,1... | collective-permute-start | bytes 1572872 | tf_op jit(solution)/shard_map/ppermute | solution.py:28
  306.8 6.1 collective-permute-done
  312.9 2.5 collective-permute-start.1
  315.6 6.0 collective-permute-done.1
  322.3 2.5 collective-permute-start.2
  324.8 1.4 collective-permute-start.5
  326.2 4.8 collective-permute-done.2
  330.9 2.6 collective-permute-start.3
  334.0 2.4 collective-permute-start.6
  336.4 3.5 collective-permute-done.3
  340.0 1.9 bitcast_dynamic-update-slice_fusion.6
  341.8 1.9 bitcast_dynamic-update-slice_fusion.5
  343.7 1.9 bitcast_dynamic-update-slice_fusion.4
  347.5 1.9 bitcast_dynamic-update-slice_fusion.2
  349.4 1.9 bitcast_dynamic-update-slice_fusion.1
  352.1 5.0 gather_fusion.1
  357.1 68.6 %all-gather.13.cloned.1.call-done = bf16[2048,256]{1,0:T(8,128)(2,1)} async-done(((bf16[32,256]{1,0:T(8,128)(2,1)}), bf16[2048,256]{1,0:T(8,128)(2,1)}) %all-gather.13.cloned.1.call-update) | async-done | bytes 1048592 | tf_op jit(solution)/shard_map/all_gather | solution.py:111
  425.7 3.8 multiply_reduce_fusion.1
  429.7 2.3 fusion.49
  432.0 33.4 %all-gather.17.cloned.1.call-done = bf16[1024,512]{1,0:T(8,128)(2,1)} async-done(((bf16[128,512]{1,0:T(8,128)(2,1)}), bf16[1024,512]{1,0:T(8,128)(2,1)}) %all-gather.17.cloned.1.call-update) | async-done | bytes 1048592 | tf_op jit(solution)/shard_map/all_gather | solution.py:133
  465.5 2.1 reshape.594
  467.6 30.8 %all-gather.11.cloned.1.call-done = bf16[1024,512]{1,0:T(8,128)(2,1)} async-done(((bf16[128,512]{1,0:T(8,128)(2,1)}), bf16[1024,512]{1,0:T(8,128)(2,1)}) %all-gather.11.cloned.1.call-update) | async-done | bytes 1048592 | tf_op jit(solution)/shard_map/all_gather | solution.py:134
  498.5 2.2 reshape.591
  500.6 2.3 constant_dynamic-slice_fusion
  502.9 3.3 constant_dynamic-slice_fusion.1
  507.2 2.0 copy-done.3
  509.2 1.5 fusion.67
  510.7 119.4 %all-gather.19.cloned.1.call-done = bf16[256,2048]{0,1:T(8,128)(2,1)} async-done(((bf16[256,32]{0,1:T(8,128)(2,1)}), bf16[256,2048]{0,1:T(8,128)(2,1)}) %all-gather.19.cloned.1.call-update) | async-done | bytes 1048592 | tf_op jit(solution)/shard_map/all_gather | solution.py:114
  630.1 7.6 convolution_convert_fusion
  637.8 4.4 sort.35
  642.8 2.5 sort.34
  646.0 40.8 %reduce-scatter.2.cloned.1.call-done = bf16[128,2048]{1,0:T(8,128)(2,1)} async-done(((bf16[1024,2048]{1,0:T(8,128)(2,1)}), bf16[128,2048]{1,0:T(8,128)(2,1)}) %reduce-scatter.2.cloned.1.call-update) | async-done | bytes 524304 | tf_op jit(solution)/shard_map/reduce_scatter | solution.py:147
  688.1 1.5 convolution_convert_fusion.1
  689.5 24.1 %psum.7 = bf16[4,2048]{1,0:T(4,128)(2,1)} all-reduce(bf16[4,2048]{1,0:T(4,128)(2,1)S(1)} %convolution_convert_fusion.1), channel_id=1, replica_groups=mesh['grp'=64,'seq'=8] {'seq'}, use_global_device_ids=true, to_apply=%region_12.14 | all-reduce | flops 8192 | bytes 32768 | tf_op jit(solution)/shard_map/psum | solution.py:174
  715.0 3.2 pad_maximum_fusion
  718.2 2.9 gather_fusion.4
  723.0 122.1 %all-gather.21.cloned.1.call-done = bf16[64,4,2048]{2,1,0:T(4,128)(2,1)} async-done(((bf16[1,4,2048]{2,1,0:T(4,128)(2,1)}), bf16[64,4,2048]{2,1,0:T(4,128)(2,1)}) %all-gather.21.cloned.1.call-update) | async-done | bytes 1048592 | tf_op jit(solution)/shard_map/all_gather | solution.py:175
  845.0 2.5 reshape.703
  847.5 1.8 multiply_reduce_fusion
  849.9 2.4 fusion.10
  852.3 110.0 %pmax.7 = f32[256]{0:T(256)} all-reduce(f32[256]{0:T(256)S(1)} %fusion.10), channel_id=1, replica_groups=mesh['grp'=64,'seq'=8] {'grp','seq'}, use_global_device_ids=true, to_apply=%region_15.17 | all-reduce | flops 256 | bytes 2048 | tf_op jit(solution)/shard_map/pmax | solution.py:182
  (99 shorter events, 18.9 us)
Async XLA Ops:
  7.2 842.7 %copy-start = (bf16[512,2048]{1,0:T(8,128)(2,1)S(1)}, bf16[512,2048]{1,0:T(8,128)(2,1)}, u32[]{:S(2)}) copy-start(bf16[512,2048]{1,0:T(8,128)(2,1)} %param.29) | copy-start | bytes 6291460
  7.2 9.6 copy-start.1
  7.2 9.6 copy-start.6
  7.2 10.2 %copy-start.2 = (bf16[1,128,2048]{2,1,0:T(8,128)(2,1)S(1)}, bf16[1,128,2048]{2,1,0:T(8,128)(2,1)}, u32[]{:S(2)}) copy-start(bf16[1,128,2048]{2,1,0:T(8,128)(2,1)} %param.16) | copy-start | bytes 1572868
  7.2 141.2 %all-gather.15.cloned.1.call-start = ((), (), s32[]{:S(2)}) async-start(), calls=%async_computation.4 | async-start | bytes 2129920 | tf_op jit(solution)/shard_map/all_gather | solution.py:112
  7.9 280.5 %all-gather.9.cloned.1.call-start = ((), (), s32[]{:S(2)}) async-start(), calls=%async_computation.1 | async-start | bytes 2129920 | tf_op jit(solution)/shard_map/all_gather | solution.py:113
  8.7 417.0 %all-gather.13.cloned.1.call-start = ((), (), s32[]{:S(2)}) async-start(), calls=%async_computation.3 | async-start | bytes 1064960 | tf_op jit(solution)/shard_map/all_gather | solution.py:111
  9.4 456.0 %all-gather.17.cloned.1.call-start = ((), (), s32[]{:S(2)}) async-start(), calls=%async_computation.5 | async-start | bytes 1179648 | tf_op jit(solution)/shard_map/all_gather | solution.py:133
  11.0 141.4 %copy-start.7 = (f32[2048]{0:T(1024)S(1)}, f32[2048]{0:T(1024)}, u32[]{:S(2)}) copy-start(f32[2048]{0:T(1024)} %param.20) | copy-start | bytes 24580
  16.7 138.2 %copy-start.9 = (f32[256]{0:T(256)S(1)}, f32[256]{0:T(256)}, u32[]{:S(2)}) copy-start(f32[256]{0:T(256)} %param.25) | copy-start | bytes 3076
  156.0 342.4 %all-gather.11.cloned.1.call-start = ((), (), s32[]{:S(2)}) async-start(), calls=%async_computation.2 | async-start | bytes 1179648 | tf_op jit(solution)/shard_map/all_gather | solution.py:134
  295.9 334.2 %all-gather.19.cloned.1.call-start = ((), (), s32[]{:S(2)}) async-start(), calls=%async_computation.6 | async-start | bytes 1064960 | tf_op jit(solution)/shard_map/all_gather | solution.py:114
  296.2 16.8 %collective-permute-start = (bf16[128,2048]{1,0:T(8,128)(2,1)S(1)}, bf16[128,2048]{1,0:T(8,128)(2,1)S(1)}, u32[]{:S(2)}, u32[]{:S(2)}) collective-permute-start(bf16[128,2048]{1,0:T(8,128)(2,1)S(1)} %fusion.15), channel_id=1, source_target_pairs={{0,1},{1,2},{2,3},{3,4},{4,5},{5,6},{6,7},{7,0},{8,9},{9,10},{10,1... | collective-permute-start | bytes 1572872 | tf_op jit(solution)/shard_map/ppermute | solution.py:28
  312.9 8.6 collective-permute-start.1
  315.4 9.4 collective-permute-start.4
  321.5 0.8 copy-start.5
  322.3 8.6 collective-permute-start.2
  324.8 9.2 collective-permute-start.5
  330.9 9.0 collective-permute-start.3
  333.6 353.2 %reduce-scatter.2.cloned.1.call-start = ((), (), s32[]{:S(2)}) async-start(), calls=%async_computation.7 | async-start | bytes 4718592 | tf_op jit(solution)/shard_map/reduce_scatter | solution.py:147
  334.0 17.2 %collective-permute-start.6 = (bf16[128,2048]{1,0:T(8,128)(2,1)}, bf16[128,2048]{1,0:T(8,128)(2,1)S(1)}, u32[]{:S(2)}, u32[]{:S(2)}) collective-permute-start(bf16[128,2048]{1,0:T(8,128)(2,1)} %collective-permute-done.5), channel_id=1, source_target_pairs={{1,0},{2,1},{3,2},{4,3},{5,4},{6,5},{7,6},{0,7},{9,8},{10,9},{11,1... | collective-permute-start | bytes 1572872 | tf_op jit(solution)/shard_map/ppermute | solution.py:30
  425.7 3.8 copy-start.10
  507.2 2.0 copy-start.3
  637.7 5.1 copy-start.12
  637.7 50.3 %copy-start.8 = (f32[2048]{0:T(1024)S(1)}, f32[2048]{0:T(1024)}, u32[]{:S(2)}) copy-start(f32[2048]{0:T(1024)} %param.27) | copy-start | bytes 24580
  637.8 207.3 %all-gather.21.cloned.1.call-start = ((), (), s32[]{:S(2)}) async-start(), calls=%async_computation.8 | async-start | bytes 1064960 | tf_op jit(solution)/shard_map/all_gather | solution.py:175
  688.0 33.9 %copy-start.4 = (bf16[128,2048]{1,0:T(8,128)(2,1)S(1)}, bf16[128,2048]{1,0:T(8,128)(2,1)}, u32[]{:S(2)}) copy-start(bf16[128,2048]{1,0:T(8,128)(2,1)} %reduce-scatter.2.cloned.1.call-done) | copy-start | bytes 1572868
  721.1 128.8 %copy-start.11 = (f32[2048]{0:T(1024)S(1)}, f32[2048]{0:T(1024)}, u32[]{:S(2)}) copy-start(f32[2048]{0:T(1024)} %param.28) | copy-start | bytes 24580
Sparse Core Ops, SparseCore 0:
  11.0 137.4 all-gather.14
  151.4 136.9 all-gather.8
  291.4 134.3 all-gather.12
  428.3 37.1 all-gather.16
  467.5 30.9 all-gather.10
  501.3 128.8 all-gather.18
  637.9 48.8 reduce-scatter.1
  713.8 131.2 all-gather.20
